TPU v7x, 32 devices: a whole 2x2x4 slice. The times are simulated.
32 devices in a mesh: gx: 4 (over z), gy: 2 (over x), gz: 4 (over y, core).
Axes of the slice: x: 2, y: 2, z: 4, core: 2. Of those that a mesh axis runs over, the one named last changes fastest.
Arguments:
- loads: float32 [4, 2, 4, 1024, 128], P('gx', 'gy', 'gz'), may hold values from -12 to 12
- start: float32 [4, 2, 4, 1024, 128], P('gx', 'gy', 'gz'), may hold values from -6 to 6
- schur: float32 [4, 2, 4, 1024, 1024], P('gx', 'gy', 'gz'), may hold values from -2 to 8
- inv_local: float32 [4, 2, 4, 1024, 1024], P('gx', 'gy', 'gz'), may hold values from -1 to 3
- basis: float32 [4, 2, 4, 1024, 128], P('gx', 'gy', 'gz'), may hold values from -0.1875 to 0.1875
- coarse_inv: float32 [4096, 4096], P(('gx', 'gy')), may hold values from -0.01 to 0.07
- face_index: int32 [4, 2, 4, 6, 160], P('gx', 'gy', 'gz'), may hold values from 0 to 1023, as said below
- multiplicity: int32 [4, 2, 4, 1024], P('gx', 'gy', 'gz'), may hold values from 1 to 2, as said below
- primal_map: int32 [4, 2, 4, 128], P('gx', 'gy', 'gz'), may hold values from 0 to 4095, all different within a row
Outputs:
- solution: float32 [4, 2, 4, 1024, 128], P('gx', 'gy', 'gz')
- residual: float32 [4, 2, 4, 1024, 128], P('gx', 'gy', 'gz')
Inputs may be any that keep to these rules, and one draw needn't show every extreme that they name: face_index[x, y, z, 2a + s] lists 160 distinct interface slots of subdomain (x, y, z) on its face toward the lower (s = 0) or higher (s = 1) neighbour along grid direction a; the six lists of one subdomain are disjoint. `multiplicity`: 1, plus 1 on slots listed in a face whose neighbouring subdomain lies inside the grid. `primal_map`: each subdomain lists 128 distinct primal unknowns, and every primal unknown is listed by some subdomain.
All inputs are finite; a program needn't handle non-finite values.
Results may differ from a plain program's by a relative error of at most 0.00012.
Values sent between devices are 32-bit elements; how exact they have to be, the bound alone decides.
A program may use at most 64 MiB of HBM per device.

v0:
```python
import jax
import jax.numpy as jnp
from jax import lax
from jax.sharding import PartitionSpec as P

ITERS = 2


damping = 0.6


def extended(block, sides, width):
    for axis, dim in sides:
        count = lax.axis_size(axis)
        forward = [(i, i + 1) for i in range(count - 1)]
        backward = [(target, source) for source, target in forward]
        low = lax.ppermute(
            lax.slice_in_dim(block, block.shape[dim] - width, None, axis=dim), axis, forward
        )
        high = lax.ppermute(lax.slice_in_dim(block, 0, width, axis=dim), axis, backward)
        block = jnp.concatenate([low, block, high], axis=dim)
    return block


def precise(matrix, vectors):
    return jnp.dot(
        matrix, vectors, precision=lax.Precision.HIGHEST, preferred_element_type=jnp.float32
    )


def interface_sum(field, slots):
    face_values = field[slots]
    along_first = extended(face_values[0:2], (("gx", 0),), 1)
    along_second = extended(face_values[2:4], (("gy", 0),), 1)
    along_third = extended(face_values[4:6], (("gz", 0),), 1)
    arrived = jnp.stack(
        [
            along_first[0],
            along_first[3],
            along_second[0],
            along_second[3],
            along_third[0],
            along_third[3],
        ]
    )
    return field.at[slots.reshape(-1)].add(arrived.reshape(-1, field.shape[1]))


def coarse_solve(coarse_rows, coarse_load):
    quarter = coarse_rows.shape[0] // lax.axis_size("gz")
    first_row = lax.axis_index("gz") * quarter
    own_rows = lax.dynamic_slice_in_dim(coarse_rows, first_row, quarter, 0)
    return lax.all_gather(precise(own_rows, coarse_load), ("gx", "gy", "gz"), axis=0, tiled=True)


def body(loads, start, schur, inv_local, basis, coarse_inv, face_index, multiplicity, primal_map):
    unknowns = loads.shape[3]
    load_cases = loads.shape[4]
    load_field = loads.reshape(unknowns, load_cases)
    solution = start.reshape(unknowns, load_cases)
    stiff_matrix = schur.reshape(unknowns, unknowns)
    inverse_matrix = inv_local.reshape(unknowns, unknowns)
    modes = basis.reshape(unknowns, -1)
    slots = face_index.reshape(6, -1)
    weight = 1.0 / multiplicity.reshape(unknowns, 1).astype(jnp.float32)
    primal_ids = primal_map.reshape(-1)
    primal_total = coarse_inv.shape[1]
    residual = solution
    for iteration in range(ITERS):
        residual = load_field - interface_sum(precise(stiff_matrix, solution), slots)
        weighted = weight * residual
        local = precise(inverse_matrix, weighted)
        terms = lax.dot_general(
            modes,
            weighted,
            (((0,), (0,)), ((), ())),
            precision=lax.Precision.HIGHEST,
            preferred_element_type=jnp.float32,
        )
        coarse_local = jnp.zeros((primal_total, load_cases), jnp.float32).at[primal_ids].add(terms)
        coarse_load = lax.psum(coarse_local, ("gx", "gy", "gz"))
        coarse_sol = coarse_solve(coarse_inv, coarse_load)
        correction = precise(modes, coarse_sol[primal_ids])
        update = interface_sum(weight * (local + correction), slots)
        solution = solution + damping * update
    return (solution.reshape(loads.shape), residual.reshape(loads.shape))


def solution(mesh):
    placed = (
        P("gx", "gy", "gz", None, None),
        P("gx", "gy", "gz", None, None),
        P("gx", "gy", "gz", None, None),
        P("gx", "gy", "gz", None, None),
        P("gx", "gy", "gz", None, None),
        P(("gx", "gy"), None),
        P("gx", "gy", "gz", None, None),
        P("gx", "gy", "gz", None),
        P("gx", "gy", "gz", None),
    )
    return jax.shard_map(
        body,
        mesh=mesh,
        in_specs=placed,
        out_specs=(P("gx", "gy", "gz", None, None), P("gx", "gy", "gz", None, None)),
        check_vma=False,
    )
```

profile of v0, /device:TPU:11, one launch (start us, length us, event | category | flops | bytes accessed | tf_op | source)
XLA Modules:
  0.0 563.8 jit_solution(8171522895181699997)
XLA Ops:
  8.1 5.3 fusion.6
  13.4 2.9 gather_fusion
  16.4 3.2 collective-permute-start
  19.6 2.1 collective-permute-start.1
  21.6 1.3 collective-permute-start.2
  22.9 4.0 collective-permute-start.3
  26.9 4.8 collective-permute-start.4
  32.0 1.9 collective-permute-start.5
  34.0 3.7 collective-permute-done.5
  37.8 6.3 %scatter_fusion = f32[1024,128]{1,0:T(8,128)S(1)} fusion(f32[1024,128]{1,0:T(8,128)S(1)} %fusion.6, s32[960]{0:T(1024)S(1)} %bitcast.137, f32[960,128]{1,0:T(8,128)S(1)} %bitcast.133), kind=kCustom, calls=%fused_computation.6 | custom fusion | flops 122880 | bytes 1478400 | tf_op jit(solution)/shard_map/scatter-add | solution.py:46
  45.2 2.4 scatter_custom_fusion.1
  47.7 132.7 %all-reduce.3.cloned.1.call-done = f32[4096,128]{1,0:T(8,128)} async-done(((f32[4096,128]{1,0:T(8,128)}), f32[4096,128]{1,0:T(8,128)}) %all-reduce.3.cloned.1.call-update) | async-done | bytes 2097168 | tf_op jit(solution)/shard_map/psum | solution.py:81
  180.4 5.0 fusion.10
  185.9 55.8 %all-gather.3.cloned.1.call-done = f32[4096,128]{1,0:T(8,128)} async-done(((f32[128,128]{1,0:T(8,128)}), f32[4096,128]{1,0:T(8,128)}) %all-gather.3.cloned.1.call-update) | async-done | bytes 2097168 | tf_op jit(solution)/shard_map/all_gather | solution.py:53
  241.7 2.2 gather_fusion.1
  244.6 6.0 %fusion.27 = f32[1024,128]{0,1:T(8,128)S(1)} fusion(f32[128,1024]{1,0:T(8,128)S(1)} %fusion.40, f32[1,1,1,1024,1024]{4,3,2,1,0:T(8,128)} %param.12, f32[1024]{0:T(1024)S(1)} %bitcast.142, f32[1024,128]{1,0:T(8,128)S(1)} %scatter_fusion, f32[1,1,1,1024,128]{4,3,2,1,0:T(8,128)S(1)} %copy-done.1), kind=kOutput, calls=%fused_computation.29 | convolution fusion | flops 1611137024 | bytes 6295552 | tf_op jit(solution)/shard_map/dot_general | solution.py:26
  250.8 2.9 gather_fusion.2
  253.7 2.4 collective-permute-start.6
  256.1 2.9 collective-permute-start.7
  260.3 4.0 collective-permute-start.9
  264.3 3.7 collective-permute-start.10
  268.0 1.9 collective-permute-start.11
  270.1 3.7 collective-permute-done.11
  273.8 6.3 %scatter_fusion.1 = f32[1024,128]{1,0:T(8,128)S(1)} fusion(f32[1024,128]{1,0:T(8,128)S(1)} %copy.12, s32[960]{0:T(1024)S(1)} %bitcast.138, f32[960,128]{1,0:T(8,128)S(1)} %bitcast.134), kind=kCustom, calls=%fused_computation.8 | custom fusion | flops 122880 | bytes 1478400 | tf_op jit(solution)/shard_map/scatter-add | solution.py:46
  280.1 6.7 %fusion.30 = f32[1024,128]{0,1:T(8,128)S(1)} fusion(f32[1,1,1,1024,1024]{4,3,2,1,0:T(8,128)} %param.11, f32[1,1,1,1024,128]{4,3,2,1,0:T(8,128)S(1)} %copy-done.2, f32[1024,128]{1,0:T(8,128)S(1)} %scatter_fusion.1), kind=kOutput, calls=%fused_computation.30 | convolution fusion | flops 1610874880 | bytes 5767168 | tf_op jit(solution)/shard_map/dot_general | solution.py:26
  286.9 2.9 gather_fusion.3
  289.9 2.5 collective-permute-start.12
  292.4 2.7 collective-permute-start.13
  296.5 4.0 collective-permute-start.15
  300.5 3.1 collective-permute-start.16
  303.6 1.9 collective-permute-start.17
  305.7 3.7 collective-permute-done.17
  309.4 6.2 %scatter_fusion.2 = f32[1024,128]{1,0:T(8,128)S(1)} fusion(f32[1024,128]{1,0:T(8,128)S(1)} %copy.14, s32[960]{0:T(1024)S(1)} %bitcast.139, f32[960,128]{1,0:T(8,128)S(1)} %bitcast.135), kind=kCustom, calls=%fused_computation.9 | custom fusion | flops 122880 | bytes 1478400 | tf_op jit(solution)/shard_map/scatter-add | solution.py:46
  316.8 2.4 scatter_custom_fusion.4
  319.3 132.1 %all-reduce.5.cloned.1.call-done = f32[4096,128]{1,0:T(8,128)} async-done(((f32[4096,128]{1,0:T(8,128)}), f32[4096,128]{1,0:T(8,128)}) %all-reduce.5.cloned.1.call-update) | async-done | bytes 2097168 | tf_op jit(solution)/shard_map/psum | solution.py:81
  451.4 5.0 fusion.8
  456.4 56.3 %all-gather.5.cloned.1.call-done = f32[4096,128]{1,0:T(8,128)} async-done(((f32[128,128]{1,0:T(8,128)}), f32[4096,128]{1,0:T(8,128)}) %all-gather.5.cloned.1.call-update) | async-done | bytes 2097168 | tf_op jit(solution)/shard_map/all_gather | solution.py:53
  512.7 2.2 gather_fusion.4
  515.6 6.8 %fusion.21 = f32[1024,128]{0,1:T(8,128)} fusion(f32[128,1024]{1,0:T(8,128)S(1)} %fusion.37, f32[1,1,1,1024,1024]{4,3,2,1,0:T(8,128)} %param.12, f32[1024]{0:T(1024)S(1)} %bitcast.144, f32[1024,128]{1,0:T(8,128)S(1)} %scatter_fusion.2, f32[1,1,1,1024,128]{4,3,2,1,0:T(8,128)S(1)} %copy-done.1), kind=kOutput, calls=%fused_computation.27 | convolution fusion | flops 1611137024 | bytes 6295552 | tf_op jit(solution)/shard_map/dot_general | solution.py:26
  523.7 4.0 gather_fusion.5
  528.8 2.4 collective-permute-start.18
  532.0 2.9 collective-permute-start.19
  534.9 1.3 collective-permute-start.20
  536.2 4.2 collective-permute-start.21
  540.4 3.7 collective-permute-start.22
  544.2 1.9 collective-permute-start.23
  546.2 3.7 collective-permute-done.23
  549.9 6.2 %scatter_fusion.3 = f32[1024,128]{1,0:T(8,128)S(1)} fusion(f32[1024,128]{1,0:T(8,128)S(1)} %copy.16, s32[960]{0:T(1024)S(1)} %bitcast.140, f32[960,128]{1,0:T(8,128)S(1)} %bitcast.136), kind=kCustom, calls=%fused_computation.11 | custom fusion | flops 122880 | bytes 1478400 | tf_op jit(solution)/shard_map/scatter-add | solution.py:46
  (88 shorter events, 12.7 us)
Async XLA Ops:
  7.2 36.9 %copy-start = (f32[1,1,1,1024,128]{4,3,2,1,0:T(8,128)S(1)}, f32[1,1,1,1024,128]{4,3,2,1,0:T(8,128)}, u32[]{:S(2)}) copy-start(f32[1,1,1,1024,128]{4,3,2,1,0:T(8,128)} %param.13) | copy-start | bytes 1572868
  7.2 173.2 %all-reduce.3.cloned.1.call-start = ((), (), s32[]{:S(2)}) async-start(), calls=%async_computation | async-start | bytes 4194304 | tf_op jit(solution)/shard_map/psum | solution.py:81
  13.4 18.4 %copy-start.3 = (s32[1,1,1,6,160]{4,2,3,1,0:T(1,128)S(1)}, s32[1,1,1,6,160]{4,2,3,1,0:T(1,128)}, u32[]{:S(2)}) copy-start(s32[1,1,1,6,160]{4,2,3,1,0:T(1,128)} %param.15) | copy-start | bytes 11524
  13.4 18.5 %copy-start.4 = (s32[1,1,1,1024]{3,2,1,0:T(1,128)S(1)}, s32[1,1,1,1024]{3,2,1,0:T(1,128)}, u32[]{:S(2)}) copy-start(s32[1,1,1,1024]{3,2,1,0:T(1,128)} %param.16) | copy-start | bytes 12292
  13.4 18.5 %copy-start.5 = (s32[1,1,1,128]{3,2,1,0:T(1,128)S(1)}, s32[1,1,1,128]{3,2,1,0:T(1,128)}, u32[]{:S(2)}) copy-start(s32[1,1,1,128]{3,2,1,0:T(1,128)} %param.17) | copy-start | bytes 1540
  16.4 15.6 %collective-permute-start = (f32[1,160,128]{2,1,0:T(8,128)S(1)}, f32[1,160,128]{2,1,0:T(8,128)S(1)}, u32[]{:S(2)}, u32[]{:S(2)}) collective-permute-start(f32[1,160,128]{2,1,0:T(8,128)S(1)} %get-tuple-element.25), channel_id=1, source_target_pairs={{0,8},{8,16},{16,24},{1,9},{9,17},{17,25},{2,10},{10,18},{18,26},{... | collective-permute-start | bytes 245768 | tf_op jit(solution)/shard_map/ppermute | solution.py:17
  19.6 14.4 %collective-permute-start.1 = (f32[1,160,128]{2,1,0:T(8,128)S(1)}, f32[1,160,128]{2,1,0:T(8,128)S(1)}, u32[]{:S(2)}, u32[]{:S(2)}) collective-permute-start(f32[1,160,128]{2,1,0:T(8,128)S(1)} %get-tuple-element.24), channel_id=1, source_target_pairs={{8,0},{16,8},{24,16},{9,1},{17,9},{25,17},{10,2},{18,10},{26,18},{... | collective-permute-start | bytes 245768 | tf_op jit(solution)/shard_map/ppermute | solution.py:20
  21.6 12.3 %collective-permute-start.2 = (f32[1,160,128]{2,1,0:T(8,128)S(1)}, f32[1,160,128]{2,1,0:T(8,128)S(1)}, u32[]{:S(2)}, u32[]{:S(2)}) collective-permute-start(f32[1,160,128]{2,1,0:T(8,128)S(1)} %get-tuple-element.23), channel_id=1, source_target_pairs={{0,4},{1,5},{2,6},{3,7},{8,12},{9,13},{10,14},{11,15},{16,20},{17,... | collective-permute-start | bytes 245768 | tf_op jit(solution)/shard_map/ppermute | solution.py:17
  22.9 11.0 %collective-permute-start.3 = (f32[1,160,128]{2,1,0:T(8,128)S(1)}, f32[1,160,128]{2,1,0:T(8,128)S(1)}, u32[]{:S(2)}, u32[]{:S(2)}) collective-permute-start(f32[1,160,128]{2,1,0:T(8,128)S(1)} %get-tuple-element.22), channel_id=1, source_target_pairs={{4,0},{5,1},{6,2},{7,3},{12,8},{13,9},{14,10},{15,11},{20,16},{21,... | collective-permute-start | bytes 245768 | tf_op jit(solution)/shard_map/ppermute | solution.py:20
  26.9 7.1 %collective-permute-start.4 = (f32[1,160,128]{2,1,0:T(8,128)S(1)}, f32[1,160,128]{2,1,0:T(8,128)S(1)}, u32[]{:S(2)}, u32[]{:S(2)}) collective-permute-start(f32[1,160,128]{2,1,0:T(8,128)S(1)} %get-tuple-element.21), channel_id=1, source_target_pairs={{0,1},{1,2},{2,3},{4,5},{5,6},{6,7},{8,9},{9,10},{10,11},{12,13},{... | collective-permute-start | bytes 245768 | tf_op jit(solution)/shard_map/ppermute | solution.py:17
  32.0 5.8 %collective-permute-start.5 = (f32[1,160,128]{2,1,0:T(8,128)S(1)}, f32[1,160,128]{2,1,0:T(8,128)S(1)}, u32[]{:S(2)}, u32[]{:S(2)}) collective-permute-start(f32[1,160,128]{2,1,0:T(8,128)S(1)} %get-tuple-element.20), channel_id=1, source_target_pairs={{1,0},{2,1},{3,2},{5,4},{6,5},{7,6},{9,8},{10,9},{11,10},{13,12},{... | collective-permute-start | bytes 245768 | tf_op jit(solution)/shard_map/ppermute | solution.py:20
  37.7 6.3 %copy-start.1 = (f32[1,1,1,1024,128]{4,3,2,1,0:T(8,128)S(1)}, f32[1,1,1,1024,128]{4,3,2,1,0:T(8,128)}, u32[]{:S(2)}) copy-start(f32[1,1,1,1024,128]{4,3,2,1,0:T(8,128)} %param.9) | copy-start | bytes 1572868
  47.6 194.0 %all-gather.3.cloned.1.call-start = ((), (), s32[]{:S(2)}) async-start(), calls=%async_computation.1 | async-start | bytes 2162688 | tf_op jit(solution)/shard_map/all_gather | solution.py:53
  185.4 266.0 %all-reduce.5.cloned.1.call-start = ((), (), s32[]{:S(2)}) async-start(), calls=%async_computation.2 | async-start | bytes 4194304 | tf_op jit(solution)/shard_map/psum | solution.py:81
  253.7 14.3 %collective-permute-start.6 = (f32[1,160,128]{2,1,0:T(8,128)S(1)}, f32[1,160,128]{2,1,0:T(8,128)S(1)}, u32[]{:S(2)}, u32[]{:S(2)}) collective-permute-start(f32[1,160,128]{2,1,0:T(8,128)S(1)} %get-tuple-element.19), channel_id=1, source_target_pairs={{0,8},{8,16},{16,24},{1,9},{9,17},{17,25},{2,10},{10,18},{18,26},{... | collective-permute-start | bytes 245768 | tf_op jit(solution)/shard_map/ppermute | solution.py:17
  256.1 13.9 %collective-permute-start.7 = (f32[1,160,128]{2,1,0:T(8,128)S(1)}, f32[1,160,128]{2,1,0:T(8,128)S(1)}, u32[]{:S(2)}, u32[]{:S(2)}) collective-permute-start(f32[1,160,128]{2,1,0:T(8,128)S(1)} %get-tuple-element.18), channel_id=1, source_target_pairs={{8,0},{16,8},{24,16},{9,1},{17,9},{25,17},{10,2},{18,10},{26,18},{... | collective-permute-start | bytes 245768 | tf_op jit(solution)/shard_map/ppermute | solution.py:20
  259.0 11.0 %collective-permute-start.8 = (f32[1,160,128]{2,1,0:T(8,128)S(1)}, f32[1,160,128]{2,1,0:T(8,128)S(1)}, u32[]{:S(2)}, u32[]{:S(2)}) collective-permute-start(f32[1,160,128]{2,1,0:T(8,128)S(1)} %get-tuple-element.17), channel_id=1, source_target_pairs={{0,4},{1,5},{2,6},{3,7},{8,12},{9,13},{10,14},{11,15},{16,20},{17,... | collective-permute-start | bytes 245768 | tf_op jit(solution)/shard_map/ppermute | solution.py:17
  260.3 9.7 %collective-permute-start.9 = (f32[1,160,128]{2,1,0:T(8,128)S(1)}, f32[1,160,128]{2,1,0:T(8,128)S(1)}, u32[]{:S(2)}, u32[]{:S(2)}) collective-permute-start(f32[1,160,128]{2,1,0:T(8,128)S(1)} %get-tuple-element.16), channel_id=1, source_target_pairs={{4,0},{5,1},{6,2},{7,3},{12,8},{13,9},{14,10},{15,11},{20,16},{21,... | collective-permute-start | bytes 245768 | tf_op jit(solution)/shard_map/ppermute | solution.py:20
  264.3 5.7 %collective-permute-start.10 = (f32[1,160,128]{2,1,0:T(8,128)S(1)}, f32[1,160,128]{2,1,0:T(8,128)S(1)}, u32[]{:S(2)}, u32[]{:S(2)}) collective-permute-start(f32[1,160,128]{2,1,0:T(8,128)S(1)} %get-tuple-element.15), channel_id=1, source_target_pairs={{0,1},{1,2},{2,3},{4,5},{5,6},{6,7},{8,9},{9,10},{10,11},{12,13},{... | collective-permute-start | bytes 245768 | tf_op jit(solution)/shard_map/ppermute | solution.py:17
  268.0 5.8 %collective-permute-start.11 = (f32[1,160,128]{2,1,0:T(8,128)S(1)}, f32[1,160,128]{2,1,0:T(8,128)S(1)}, u32[]{:S(2)}, u32[]{:S(2)}) collective-permute-start(f32[1,160,128]{2,1,0:T(8,128)S(1)} %get-tuple-element.14), channel_id=1, source_target_pairs={{1,0},{2,1},{3,2},{5,4},{6,5},{7,6},{9,8},{10,9},{11,10},{13,12},{... | collective-permute-start | bytes 245768 | tf_op jit(solution)/shard_map/ppermute | solution.py:20
  273.8 6.3 %copy-start.2 = (f32[1,1,1,1024,128]{4,3,2,1,0:T(8,128)S(1)}, f32[1,1,1,1024,128]{4,3,2,1,0:T(8,128)}, u32[]{:S(2)}) copy-start(f32[1,1,1,1024,128]{4,3,2,1,0:T(8,128)} %param.10) | copy-start | bytes 1572868
  289.9 13.7 %collective-permute-start.12 = (f32[1,160,128]{2,1,0:T(8,128)S(1)}, f32[1,160,128]{2,1,0:T(8,128)S(1)}, u32[]{:S(2)}, u32[]{:S(2)}) collective-permute-start(f32[1,160,128]{2,1,0:T(8,128)S(1)} %get-tuple-element.13), channel_id=1, source_target_pairs={{0,8},{8,16},{16,24},{1,9},{9,17},{17,25},{2,10},{10,18},{18,26},{... | collective-permute-start | bytes 245768 | tf_op jit(solution)/shard_map/ppermute | solution.py:17
  292.4 13.1 %collective-permute-start.13 = (f32[1,160,128]{2,1,0:T(8,128)S(1)}, f32[1,160,128]{2,1,0:T(8,128)S(1)}, u32[]{:S(2)}, u32[]{:S(2)}) collective-permute-start(f32[1,160,128]{2,1,0:T(8,128)S(1)} %get-tuple-element.12), channel_id=1, source_target_pairs={{8,0},{16,8},{24,16},{9,1},{17,9},{25,17},{10,2},{18,10},{26,18},{... | collective-permute-start | bytes 245768 | tf_op jit(solution)/shard_map/ppermute | solution.py:20
  295.2 10.4 %collective-permute-start.14 = (f32[1,160,128]{2,1,0:T(8,128)S(1)}, f32[1,160,128]{2,1,0:T(8,128)S(1)}, u32[]{:S(2)}, u32[]{:S(2)}) collective-permute-start(f32[1,160,128]{2,1,0:T(8,128)S(1)} %get-tuple-element.11), channel_id=1, source_target_pairs={{0,4},{1,5},{2,6},{3,7},{8,12},{9,13},{10,14},{11,15},{16,20},{17,... | collective-permute-start | bytes 245768 | tf_op jit(solution)/shard_map/ppermute | solution.py:17
  296.5 9.2 %collective-permute-start.15 = (f32[1,160,128]{2,1,0:T(8,128)S(1)}, f32[1,160,128]{2,1,0:T(8,128)S(1)}, u32[]{:S(2)}, u32[]{:S(2)}) collective-permute-start(f32[1,160,128]{2,1,0:T(8,128)S(1)} %get-tuple-element.10), channel_id=1, source_target_pairs={{4,0},{5,1},{6,2},{7,3},{12,8},{13,9},{14,10},{15,11},{20,16},{21,... | collective-permute-start | bytes 245768 | tf_op jit(solution)/shard_map/ppermute | solution.py:20
  300.5 5.2 collective-permute-start.16
  303.6 5.8 %collective-permute-start.17 = (f32[1,160,128]{2,1,0:T(8,128)S(1)}, f32[1,160,128]{2,1,0:T(8,128)S(1)}, u32[]{:S(2)}, u32[]{:S(2)}) collective-permute-start(f32[1,160,128]{2,1,0:T(8,128)S(1)} %get-tuple-element.8), channel_id=1, source_target_pairs={{1,0},{2,1},{3,2},{5,4},{6,5},{7,6},{9,8},{10,9},{11,10},{13,12},{... | collective-permute-start | bytes 245768 | tf_op jit(solution)/shard_map/ppermute | solution.py:20
  319.2 193.5 %all-gather.5.cloned.1.call-start = ((), (), s32[]{:S(2)}) async-start(), calls=%async_computation.3 | async-start | bytes 2162688 | tf_op jit(solution)/shard_map/all_gather | solution.py:53
  528.8 15.4 %collective-permute-start.18 = (f32[1,160,128]{2,1,0:T(8,128)S(1)}, f32[1,160,128]{2,1,0:T(8,128)S(1)}, u32[]{:S(2)}, u32[]{:S(2)}) collective-permute-start(f32[1,160,128]{2,1,0:T(8,128)S(1)} %get-tuple-element.7), channel_id=1, source_target_pairs={{0,8},{8,16},{16,24},{1,9},{9,17},{17,25},{2,10},{10,18},{18,26},{... | collective-permute-start | bytes 245768 | tf_op jit(solution)/shard_map/ppermute | solution.py:17
  532.0 14.1 %collective-permute-start.19 = (f32[1,160,128]{2,1,0:T(8,128)S(1)}, f32[1,160,128]{2,1,0:T(8,128)S(1)}, u32[]{:S(2)}, u32[]{:S(2)}) collective-permute-start(f32[1,160,128]{2,1,0:T(8,128)S(1)} %get-tuple-element.6), channel_id=1, source_target_pairs={{8,0},{16,8},{24,16},{9,1},{17,9},{25,17},{10,2},{18,10},{26,18},{... | collective-permute-start | bytes 245768 | tf_op jit(solution)/shard_map/ppermute | solution.py:20
  534.9 11.2 %collective-permute-start.20 = (f32[1,160,128]{2,1,0:T(8,128)S(1)}, f32[1,160,128]{2,1,0:T(8,128)S(1)}, u32[]{:S(2)}, u32[]{:S(2)}) collective-permute-start(f32[1,160,128]{2,1,0:T(8,128)S(1)} %get-tuple-element.5), channel_id=1, source_target_pairs={{0,4},{1,5},{2,6},{3,7},{8,12},{9,13},{10,14},{11,15},{16,20},{17,... | collective-permute-start | bytes 245768 | tf_op jit(solution)/shard_map/ppermute | solution.py:17
  536.2 9.9 %collective-permute-start.21 = (f32[1,160,128]{2,1,0:T(8,128)S(1)}, f32[1,160,128]{2,1,0:T(8,128)S(1)}, u32[]{:S(2)}, u32[]{:S(2)}) collective-permute-start(f32[1,160,128]{2,1,0:T(8,128)S(1)} %get-tuple-element.4), channel_id=1, source_target_pairs={{4,0},{5,1},{6,2},{7,3},{12,8},{13,9},{14,10},{15,11},{20,16},{21,... | collective-permute-start | bytes 245768 | tf_op jit(solution)/shard_map/ppermute | solution.py:20
  540.4 5.7 %collective-permute-start.22 = (f32[1,160,128]{2,1,0:T(8,128)S(1)}, f32[1,160,128]{2,1,0:T(8,128)S(1)}, u32[]{:S(2)}, u32[]{:S(2)}) collective-permute-start(f32[1,160,128]{2,1,0:T(8,128)S(1)} %get-tuple-element.3), channel_id=1, source_target_pairs={{0,1},{1,2},{2,3},{4,5},{5,6},{6,7},{8,9},{9,10},{10,11},{12,13},{... | collective-permute-start | bytes 245768 | tf_op jit(solution)/shard_map/ppermute | solution.py:17
  544.2 5.8 %collective-permute-start.23 = (f32[1,160,128]{2,1,0:T(8,128)S(1)}, f32[1,160,128]{2,1,0:T(8,128)S(1)}, u32[]{:S(2)}, u32[]{:S(2)}) collective-permute-start(f32[1,160,128]{2,1,0:T(8,128)S(1)} %get-tuple-element.2), channel_id=1, source_target_pairs={{1,0},{2,1},{3,2},{5,4},{6,5},{7,6},{9,8},{10,9},{11,10},{13,12},{... | collective-permute-start | bytes 245768 | tf_op jit(solution)/shard_map/ppermute | solution.py:20
Sparse Core Ops, SparseCore 0:
  47.8 132.5 all-reduce.2
  185.5 56.1 all-gather.2
  319.4 131.9 all-reduce.4
  456.5 56.1 all-gather.4
where the time goes:
time: 572 us; the launch traced here: 564 us
  waiting for transfers between devices  392 us (69%)
  starting transfers between devices  66.1 us (12%)
  matrix products  38.4 us (7%)
  other arithmetic  32.4 us (6%)
  local copies, waits for them, and re-layouts  20.3 us (4%)
  between operations  14.8 us (3%)
    psum x2, waiting for transfers between devices, body(): coarse_load = lax.psum(coarse_local, ('gx', 'gy', 'gz'))  265 us
    all_gather x2, waiting for transfers between devices, coarse_solve(): lax.all_gather(precise(own_rows, coarse_load), ('gx', 'gy', 'gz'), axis=0...  112 us
    dot_general x8, matrix products, precise(): jnp.dot(matrix, vectors, precision=lax.Precision.HIGHEST, preferred_eleme...  36 us
    ppermute x12, starting transfers between devices, extended(): lax.ppermute(lax.slice_in_dim(block, 0, width, axis=dim), axis, backward)  34.5 us
    ppermute x12, starting transfers between devices, extended(): lax.ppermute(lax.slice_in_dim(block, block.shape[dim] - width, None, axis...  31 us
    scatter-add x4, other arithmetic, interface_sum(): return field.at[slots.reshape(-1)].add(arrived.reshape(-1, field.shape[1]))  25 us
    ppermute x12, waiting for transfers between devices, extended(): lax.ppermute(lax.slice_in_dim(block, 0, width, axis=dim), axis, backward)  14.9 us
    gather x4, local copies, waits for them, and re-layouts, interface_sum(): face_values = field[slots]  12.7 us
  transfers between devices with their start and end apart: 28, of which 8 were waited for; matrix products, arithmetic and copies ran while one was open for 0% of the time, Pallas kernels for 0%

commit v1 on v0

v1 whole, which is shorter than its diff:
```python
import functools
import itertools

import jax
import jax.numpy as jnp
from jax import lax
from jax.experimental import pallas as pl
from jax.experimental.pallas import tpu as pltpu
from jax.sharding import PartitionSpec as P

ITERS = 2
damping = 0.6
MESH = pl.DeviceIdType.MESH
AXES = ("gx", "gy", "gz")


class Grid:
    def __init__(self, sizes):
        self.sizes = sizes
        gx, gy, gz = sizes
        self.lo = 2 if gz % 2 == 0 else 1
        self.hi = gz // self.lo
        self.stages = (gx, gy, self.hi, self.lo)
        self.count = gx * gy * gz
        self.c = tuple(lax.axis_index(a) for a in AXES)
        self.place = (self.c[0], self.c[1], self.c[2] // self.lo, self.c[2] % self.lo)

    def linear(self, place):
        x, y, h, l = place
        return (x * self.sizes[1] + y) * self.sizes[2] + h * self.lo + l

    def device(self, place):
        x, y, h, l = place
        return (x, y, h * self.lo + l)

    def barrier(self):
        semaphore = pltpu.get_barrier_semaphore()
        total = 0
        for axis in range(3):
            for delta in range(1, self.sizes[axis]):
                target = list(self.c)
                target[axis] = (self.c[axis] + delta) % self.sizes[axis]
                pl.semaphore_signal(
                    semaphore, inc=1, device_id=tuple(target), device_id_type=MESH
                )
                total += 1
        if total:
            pl.semaphore_wait(semaphore, total)


class Gather:
    def __init__(self, grid, buffer, rows, send, recv):
        self.grid, self.buffer, self.rows = grid, buffer, rows
        self.send, self.recv = send, recv
        self.sent = []

    def block(self, offset):
        g = self.grid
        place = tuple((c + n - d) % n for c, d, n in zip(g.place, offset, g.stages))
        return self.buffer.at[pl.ds(g.linear(place) * self.rows, self.rows)]

    def number(self, offset):
        value = 0
        for d, n in zip(offset, self.grid.stages):
            value = value * n + d
        return value

    def copy(self, offset, stage, delta):
        g = self.grid
        arrived = list(offset)
        arrived[stage] = delta
        place = list(g.place)
        place[stage] = (g.place[stage] + delta) % g.stages[stage]
        block = self.block(offset)
        k = self.number(arrived)
        return pltpu.make_async_remote_copy(
            src_ref=block, dst_ref=block, send_sem=self.send.at[k], recv_sem=self.recv.at[k],
            device_id=g.device(place), device_id_type=MESH,
        )

    def forward(self, offset, first):
        for stage in range(first, 4):
            for delta in range(1, self.grid.stages[stage]):
                c = self.copy(offset, stage, delta)
                c.start()
                self.sent.append(c)

    def start(self):
        self.forward((0, 0, 0, 0), 0)

    def finish(self):
        g = self.grid
        for stage in range(4):
            earlier = [range(n) for n in g.stages[:stage]]
            for head in itertools.product(*earlier):
                for delta in range(1, g.stages[stage]):
                    arrived = tuple(head) + (delta,) + (0,) * (3 - stage)
                    block = self.block(arrived)
                    k = self.number(arrived)
                    pltpu.make_async_remote_copy(
                        src_ref=block, dst_ref=block, send_sem=self.send.at[k],
                        recv_sem=self.recv.at[k], device_id=g.c, device_id_type=MESH,
                    ).wait_recv()
                    self.forward(arrived, stage + 1)

    def drain(self):
        for c in self.sent:
            c.wait_send()


def map_kernel(sizes, own_ref, all_ref, send, recv):
    grid = Grid(sizes)
    rows = own_ref.shape[0]
    all_ref[pl.ds(grid.linear(grid.place) * rows, rows), :] = own_ref[...]
    grid.barrier()
    gather = Gather(grid, all_ref, rows, send, recv)
    gather.start()
    gather.finish()
    gather.drain()


def split(value):
    high = value.astype(jnp.bfloat16)
    low = (value - high.astype(jnp.float32)).astype(jnp.bfloat16)
    return high, low


def tile_of(total, want):
    while total % want:
        want //= 2
    return want


def split_rows(source, high, low):
    rows = source.shape[0]
    tile = tile_of(rows, 64)

    def step(i, carry):
        r = pl.ds(pl.multiple_of(i * tile, tile), tile)
        h, l = split(source[r, :])
        high[r, :] = h
        low[r, :] = l
        return carry

    lax.fori_loop(0, rows // tile, step, 0)


def split_beside(source, both):
    rows, width = source.shape
    tile = tile_of(rows, 128)

    def step(i, carry):
        r = pl.ds(pl.multiple_of(i * tile, tile), tile)
        h, l = split(source[r, :])
        both[r, 0:width] = h
        both[r, width : 2 * width] = l
        return carry

    lax.fori_loop(0, rows // tile, step, 0)


def product(high, low, both):
    width = both.shape[1] // 2
    wide = jnp.dot(high, both[...], preferred_element_type=jnp.float32)
    thin = jnp.dot(low, both[:, 0:width], preferred_element_type=jnp.float32)
    return wide[:, 0:width] + wide[:, width:] + thin


def by_rows(rows, want, function):
    tile = tile_of(rows, want)

    def step(i, carry):
        function(pl.ds(pl.multiple_of(i * tile, tile), tile))
        return carry

    lax.fori_loop(0, rows // tile, step, 0)


def take_rows(target, source, index, count, base=0):
    unroll = tile_of(count, 16)

    def step(i, carry):
        first = pl.multiple_of(i * unroll, unroll)
        for j in range(unroll):
            row = index[base + first + j]
            target[pl.ds(first + j, 1), :] = source[pl.ds(row, 1), :]
        return carry

    lax.fori_loop(0, count // unroll, step, 0)


def main_kernel(
    sizes, face,
    slots, places, own_map, all_map,
    loads, start, basis, basis_t, weight, schur, inverse, coarse_t,
    solution, residual,
    full, s_high, s_low, b_high, b_low, m_high, m_low, t_high, t_low,
    c_high, c_low, picked, field, local, moved, both, term_both, sol_both, coarse_rows,
    faces, arrived, term_all, sol_all,
    load_sem, face_send, face_recv, term_send, term_recv, sol_send, sol_recv,
):
    grid = Grid(sizes)
    unknowns, cases = start.shape
    primal = basis.shape[1]
    own = coarse_t.shape[1]
    load_s = pltpu.make_async_copy(schur, full, load_sem.at[0])
    load_b = pltpu.make_async_copy(inverse, full, load_sem.at[1])
    load_s.start()
    for landing in arrived:
        landing[...] = jnp.zeros_like(landing)
    grid.barrier()
    split_rows(basis, m_high, m_low)
    split_rows(basis_t, t_high, t_low)
    solution[...] = start[...]
    sent = []

    def face_copy(turn, d):
        axis, side = d // 2, d % 2
        target = list(grid.c)
        target[axis] = grid.c[axis] + (1 if side else -1)
        return pltpu.make_async_remote_copy(
            src_ref=faces.at[turn, pl.ds(d * face, face)],
            dst_ref=arrived[turn].at[pl.ds((d ^ 1) * face, face)],
            send_sem=face_send.at[turn, d],
            recv_sem=face_recv.at[turn, d ^ 1],
            device_id=tuple(target), device_id_type=MESH,
        )

    def exists(d):
        axis, side = d // 2, d % 2
        return grid.c[axis] < sizes[axis] - 1 if side else grid.c[axis] > 0

    def exchange_start(turn):
        for d in range(6):
            take_rows(faces.at[turn, pl.ds(d * face, face)], field, slots, face, d * face)

            @pl.when(exists(d))
            def _():
                face_copy(turn, d).start()

    def exchange_finish(turn):
        for d in range(6):

            @pl.when(exists(d))
            def _():
                block = arrived[turn].at[pl.ds(d * face, face)]
                pltpu.make_async_remote_copy(
                    src_ref=block, dst_ref=block, send_sem=face_send.at[turn, d],
                    recv_sem=face_recv.at[turn, d], device_id=grid.c, device_id_type=MESH,
                ).wait_recv()

        take_rows(moved, arrived[turn], places, unknowns)

    def exchange_drain(turn):
        for d in range(6):

            @pl.when(exists(d))
            def _():
                face_copy(turn, d).wait_send()

    gathers = []
    for iteration in range(ITERS):
        turn = 2 * iteration
        split_beside(solution, both)
        if iteration == 0:
            load_s.wait()
            split_rows(full, s_high, s_low)
            load_b.start()

        def stiff(r):
            field[r, :] = product(s_high[r, :], s_low[r, :], both)

        by_rows(unknowns, 256, stiff)
        exchange_start(turn)
        if iteration == 0:
            load_b.wait()
            split_rows(full, b_high, b_low)

            def pick(p, carry):
                take_rows(picked, coarse_t, all_map, primal, p * primal)
                h, l = split(picked[...].T)
                k = pl.ds(pl.multiple_of(p * primal, primal), primal)
                c_high[:, k] = h
                c_low[:, k] = l
                return carry

            lax.fori_loop(0, grid.count, pick, 0)
        exchange_finish(turn)

        def settle(r):
            value = loads[r, :] - (field[r, :] + moved[r, :])
            residual[r, :] = value
            scaled = weight[r, :] * value
            h, l = split(scaled)
            both[r, 0:cases] = h
            both[r, cases : 2 * cases] = l

        by_rows(unknowns, 128, settle)
        mine = pl.multiple_of(grid.linear(grid.place) * primal, primal)
        term_all[iteration, pl.ds(mine, primal), :] = product(t_high[...], t_low[...], both)
        terms = Gather(grid, term_all.at[iteration], primal, term_send.at[iteration], term_recv.at[iteration])
        terms.start()
        gathers.append(terms)

        def invert(r):
            local[r, :] = product(b_high[r, :], b_low[r, :], both)

        by_rows(unknowns, 256, invert)
        terms.finish()
        mine = pl.multiple_of(grid.linear(grid.place) * own, own)
        coarse_tile = term_both.shape[0]
        sol_all[iteration][pl.ds(mine, own), :] = jnp.zeros((own, cases), jnp.float32)

        def coarse(i, carry):
            k = pl.ds(pl.multiple_of(i * coarse_tile, coarse_tile), coarse_tile)
            split_beside(term_all.at[iteration, k], term_both)
            sol_all[iteration][pl.ds(mine, own), :] += product(c_high[:, k], c_low[:, k], term_both)
            return carry

        lax.fori_loop(0, grid.count * primal // coarse_tile, coarse, 0)
        sols = Gather(grid, sol_all[iteration], own, sol_send.at[iteration], sol_recv.at[iteration])
        sols.start()
        sols.finish()
        gathers.append(sols)
        take_rows(coarse_rows, sol_all[iteration], own_map, primal)
        split_beside(coarse_rows, sol_both)

        def correct(r):
            field[r, :] = weight[r, :] * (local[r, :] + product(m_high[r, :], m_low[r, :], sol_both))

        by_rows(unknowns, 256, correct)
        exchange_start(turn + 1)
        exchange_finish(turn + 1)

        def advance(r):
            solution[r, :] = solution[r, :] + damping * (field[r, :] + moved[r, :])

        by_rows(unknowns, 128, advance)
    for turn in range(2 * ITERS):
        exchange_drain(turn)
    for gather in gathers:
        gather.drain()


def places_of(slots, unknowns):
    count = slots.shape[0]
    hit = slots[:, None] == jnp.arange(unknowns, dtype=jnp.int32)[None, :]
    position = jnp.arange(count, dtype=jnp.int32)[:, None] - count
    return jnp.sum(jnp.where(hit, position, 0), axis=0) + count


def body(sizes, loads, start, schur, inv_local, basis, coarse_inv, face_index, multiplicity, primal_map):
    unknowns, cases = loads.shape[3:]
    face = face_index.shape[4]
    primal = basis.shape[4]
    count = sizes[0] * sizes[1] * sizes[2]
    total = coarse_inv.shape[1]
    own = coarse_inv.shape[0] // sizes[2]
    slots = face_index.reshape(-1)
    places = places_of(slots, unknowns)
    own_map = primal_map.reshape(-1)
    vmem = pl.BlockSpec(memory_space=pltpu.VMEM)
    smem = pl.BlockSpec(memory_space=pltpu.SMEM)
    anywhere = pl.BlockSpec(memory_space=pl.ANY)
    dma = pltpu.SemaphoreType.DMA
    maps = pl.pallas_call(
        functools.partial(map_kernel, sizes),
        out_shape=jax.ShapeDtypeStruct((count * 8, primal), jnp.int32),
        in_specs=[vmem],
        out_specs=vmem,
        scratch_shapes=[dma((count,)), dma((count,))],
        compiler_params=pltpu.CompilerParams(collective_id=0, has_side_effects=True),
    )(jnp.broadcast_to(own_map[None, :], (8, primal)))
    all_map = maps.reshape(count, 8, primal)[:, 0, :].reshape(-1)
    own_rows = lax.dynamic_slice_in_dim(coarse_inv, lax.axis_index("gz") * own, own, 0)
    weight = jnp.broadcast_to(
        1.0 / multiplicity.reshape(unknowns, 1).astype(jnp.float32), (unknowns, cases)
    )
    modes = basis.reshape(unknowns, primal)
    f32, bf16 = jnp.float32, jnp.bfloat16
    turns = 2 * ITERS
    coarse_tile = tile_of(count * primal, 1024)
    vec = pltpu.VMEM((unknowns, cases), f32)
    out = jax.ShapeDtypeStruct((unknowns, cases), f32)
    solution, residual = pl.pallas_call(
        functools.partial(main_kernel, sizes, face),
        out_shape=(out, out),
        in_specs=[smem] * 4 + [vmem] * 5 + [anywhere] * 2 + [vmem],
        out_specs=(vmem, vmem),
        scratch_shapes=[
            pltpu.VMEM((unknowns, unknowns), f32),
            pltpu.VMEM((unknowns, unknowns), bf16),
            pltpu.VMEM((unknowns, unknowns), bf16),
            pltpu.VMEM((unknowns, unknowns), bf16),
            pltpu.VMEM((unknowns, unknowns), bf16),
            pltpu.VMEM((unknowns, primal), bf16),
            pltpu.VMEM((unknowns, primal), bf16),
            pltpu.VMEM((primal, unknowns), bf16),
            pltpu.VMEM((primal, unknowns), bf16),
            pltpu.VMEM((own, count * primal), bf16),
            pltpu.VMEM((own, count * primal), bf16),
            pltpu.VMEM((primal, own), f32),
            vec, vec, vec,
            pltpu.VMEM((unknowns, 2 * cases), bf16),
            pltpu.VMEM((coarse_tile, 2 * cases), bf16),
            pltpu.VMEM((primal, 2 * cases), bf16),
            pltpu.VMEM((primal, cases), f32),
            pltpu.VMEM((turns, 6 * face, cases), f32),
            [pltpu.VMEM((6 * face + 8, cases), f32) for _ in range(turns)],
            pltpu.VMEM((ITERS, count * primal, cases), f32),
            [pltpu.VMEM((total, cases), f32) for _ in range(ITERS)],
            dma((2,)),
            dma((turns, 6)), dma((turns, 6)),
            dma((ITERS, count)), dma((ITERS, count)),
            dma((ITERS, count)), dma((ITERS, count)),
        ],
        compiler_params=pltpu.CompilerParams(
            collective_id=1, has_side_effects=True, vmem_limit_bytes=67043328
        ),
    )(
        slots, places, own_map, all_map,
        loads.reshape(unknowns, cases), start.reshape(unknowns, cases),
        modes, modes.T, weight,
        schur.reshape(unknowns, unknowns), inv_local.reshape(unknowns, unknowns), own_rows.T,
    )
    return (solution.reshape(loads.shape), residual.reshape(loads.shape))


def solution(mesh):
    sizes = tuple(mesh.shape[a] for a in AXES)
    field = P("gx", "gy", "gz", None, None)
    placed = (field,) * 5 + (P(("gx", "gy"), None), field, P("gx", "gy", "gz", None), P("gx", "gy", "gz", None))
    return jax.shard_map(
        functools.partial(body, sizes),
        mesh=mesh,
        in_specs=placed,
        out_specs=(field, field),
        check_vma=False,
    )
```

time: 572 us -> 147 us (0.26)
  the two profiles are of different devices: /device:TPU:11 before, /device:TPU:0 now
where the time goes in v1:
time: 147 us; the launch traced here: 146 us
  Pallas kernels  133 us (90%)
  local copies, waits for them, and re-layouts  11.6 us (8%)
    pallas_call x1, Pallas kernels, body(): pl.pallas_call(functools.partial(main_kernel, sizes, face), out_shape=(ou...  117 us
    pallas_call x1, Pallas kernels, body(): pl.pallas_call(functools.partial(map_kernel, sizes), out_shape=jax.ShapeD...  16.2 us
    unnamed x14, local copies, waits for them, and re-layouts  6.62 us

profile of v1, /device:TPU:0, one launch (start us, length us, event | category | flops | bytes accessed | tf_op | source)
XLA Modules:
  0.0 146.4 jit_solution(15587116495297111346)
XLA Ops:
  0.6 0.0 copy-start.4
  0.6 0.0 copy-start.2
  0.7 0.0 copy-start.3
  0.7 0.0 copy-start
  0.7 1.8 %constant_dynamic-slice_fusion = f32[128,4096]{1,0:T(8,128)S(1)} fusion(f32[512,4096]{1,0:T(8,128)} %param.14, s32[]{:T(128)S(6)} %select_n.8), kind=kLoop, calls=%fused_computation.5 | loop fusion | bytes 4194308 | tf_op jit(solution)/shard_map/dynamic_slice | solution.py:375
  2.5 1.9 %copy.18 = f32[128,4096]{0,1:T(8,128)} copy(f32[128,4096]{1,0:T(8,128)S(1)} %constant_dynamic-slice_fusion) | data formatting | bytes 4194304
  4.4 0.0 copy-done.4
  4.4 0.6 broadcast_in_dim.26.own_ref
  5.0 16.2 %shard_map.104 = s32[256,128]{1,0:T(8,128)} custom-call(s32[8,128]{1,0:T(8,128)} %broadcast_in_dim.26.own_ref), custom_call_target="tpu_custom_call" | custom-call | tf_op jit(solution)/shard_map/pallas_call | solution.py:366
  21.2 1.5 %slice.4 = s32[32,1,128]{2,1,0:T(1,128)} slice(s32[32,8,128]{2,1,0:T(8,128)} %bitcast.24), slice={[0:32], [0:1], [0:128]} | slice | bytes 32768 | tf_op jit(solution)/shard_map/slice | solution.py:374
  22.7 0.0 copy-done.2
  22.7 0.1 reshape.54.slots
  22.8 0.0 copy-start.1
  22.8 0.6 select_reduce_fusion
  23.5 0.6 broadcast_add_fusion.places
  24.1 0.0 copy-done.3
  24.1 1.0 broadcast_in_dim.27.weight
  25.1 0.0 copy-done
  25.1 1.0 copy.14
  26.1 0.0 copy-done.1
  26.1 116.6 %shard_map.105 = (f32[1024,128]{1,0:T(8,128)}, f32[1024,128]{1,0:T(8,128)}) custom-call(s32[960]{0:T(1024)} %copy-done.1, s32[1024]{0:T(1024)} %broadcast_add_fusion.places, s32[128]{0:T(128)} %bitcast.27, s32[4096]{0:T(1024)} %bitcast.25, f32[1024,128]{1,0:T(8,128)} %bitcast.20, f32[1024,128]{1,0:T(8,128)} %bitcast.21, f32[1024,128]{1,0:T(8,128)} %bitcast.18, ...), custom_call_target="tpu_custom_call" | custom-call | tf_op jit(solution)/shard_map/pallas_call | solution.py:385
  142.7 1.9 %copy.21 = f32[1,1,1,1024,128]{4,3,2,1,0:T(8,128)} copy(f32[1,1,1,1024,128]{4,3,2,1,0:T(8,128)} %bitcast.23) | data formatting | bytes 1048576
  144.6 1.9 %copy.22 = f32[1,1,1,1024,128]{4,3,2,1,0:T(8,128)} copy(f32[1,1,1,1024,128]{4,3,2,1,0:T(8,128)} %bitcast.22) | data formatting | bytes 1048576
  (3 shorter events, 0.0 us)
Async XLA Ops:
  0.6 3.7 %copy-start.4 = (s32[1,1,1,128]{3,2,1,0:T(1,128)S(1)}, s32[1,1,1,128]{3,2,1,0:T(1,128)}, u32[]{:S(2)}) copy-start(s32[1,1,1,128]{3,2,1,0:T(1,128)} %param.17) | copy-start | bytes 1540
  0.6 22.1 %copy-start.2 = (s32[1,1,1,6,160]{4,2,3,1,0:T(1,128)S(1)}, s32[1,1,1,6,160]{4,2,3,1,0:T(1,128)}, u32[]{:S(2)}) copy-start(s32[1,1,1,6,160]{4,2,3,1,0:T(1,128)} %param.15) | copy-start | bytes 11524
  0.7 23.4 %copy-start.3 = (s32[1,1,1,1024]{3,2,1,0:T(1,128)S(1)}, s32[1,1,1,1024]{3,2,1,0:T(1,128)}, u32[]{:S(2)}) copy-start(s32[1,1,1,1024]{3,2,1,0:T(1,128)} %param.16) | copy-start | bytes 12292
  0.7 24.4 %copy-start = (f32[1,1,1,1024,128]{4,3,2,1,0:T(8,128)S(1)}, f32[1,1,1,1024,128]{4,3,2,1,0:T(8,128)}, u32[]{:S(2)}) copy-start(f32[1,1,1,1024,128]{4,3,2,1,0:T(8,128)} %param.13) | copy-start | bytes 1572868
  22.8 3.3 %copy-start.1 = (s32[960]{0:T(1024)}, s32[960]{0:T(1024)S(1)}, u32[]{:S(2)}) copy-start(s32[960]{0:T(1024)S(1)} %reshape.54.slots) | copy-start | bytes 11524

commit v2 on v1

--- a/solution.py
+++ b/solution.py
@@ -49,74 +49,89 @@
 
 
 class Gather:
-    def __init__(self, grid, buffer, rows, send, recv):
-        self.grid, self.buffer, self.rows = grid, buffer, rows
-        self.send, self.recv = send, recv
-        self.sent = []
+    def __init__(self, grid, buffer, whole, band, order, send, recv):
+        self.grid, self.buffer, self.whole, self.band = grid, buffer, whole, band
+        self.order, self.send, self.recv = order, send, recv
+        self.lengths = tuple(grid.stages[o] for o in order)
+
+    def place(self, offset):
+        g = self.grid
+        place = list(g.place)
+        for o, d in zip(self.order, offset):
+            if d:
+                place[o] = (g.place[o] + g.stages[o] - d) % g.stages[o]
+        return place
 
     def block(self, offset):
-        g = self.grid
-        place = tuple((c + n - d) % n for c, d, n in zip(g.place, offset, g.stages))
-        return self.buffer.at[pl.ds(g.linear(place) * self.rows, self.rows)]
+        first = self.grid.linear(self.place(offset)) * self.whole + self.band[0]
+        return self.buffer.at[pl.ds(pl.multiple_of(first, 8), self.band[1])]
 
     def number(self, offset):
         value = 0
-        for d, n in zip(offset, self.grid.stages):
+        for d, n in zip(offset, self.lengths):
             value = value * n + d
         return value
 
-    def copy(self, offset, stage, delta):
-        g = self.grid
-        arrived = list(offset)
-        arrived[stage] = delta
-        place = list(g.place)
-        place[stage] = (g.place[stage] + delta) % g.stages[stage]
-        block = self.block(offset)
-        k = self.number(arrived)
-        return pltpu.make_async_remote_copy(
-            src_ref=block, dst_ref=block, send_sem=self.send.at[k], recv_sem=self.recv.at[k],
-            device_id=g.device(place), device_id_type=MESH,
-        )
-
     def forward(self, offset, first):
         for stage in range(first, 4):
-            for delta in range(1, self.grid.stages[stage]):
-                c = self.copy(offset, stage, delta)
+            for delta in range(1, self.lengths[stage]):
+                back = [0, 0, 0, 0]
+                back[stage] = self.lengths[stage] - delta
+                arrived = list(offset)
+                arrived[stage] = delta
+                k = self.number(arrived)
+                block = self.block(offset)
+                c = pltpu.make_async_remote_copy(
+                    src_ref=block, dst_ref=block, send_sem=self.send,
+                    recv_sem=self.recv.at[k], device_id=self.grid.device(self.place(back)),
+                    device_id_type=MESH,
+                )
                 c.start()
-                self.sent.append(c)
 
     def start(self):
         self.forward((0, 0, 0, 0), 0)
 
+    def finish(self, stage):
+        for head in itertools.product(*[range(n) for n in self.lengths[:stage]]):
+            for delta in range(1, self.lengths[stage]):
+                arrived = tuple(head) + (delta,) + (0,) * (3 - stage)
+                block = self.block(arrived)
+                k = self.number(arrived)
+                pltpu.make_async_remote_copy(
+                    src_ref=block, dst_ref=block, send_sem=self.send,
+                    recv_sem=self.recv.at[k], device_id=self.grid.c, device_id_type=MESH,
+                ).wait_recv()
+                self.forward(arrived, stage + 1)
+
+    def drain(self):
+        if self.grid.count > 1:
+            block = self.buffer.at[pl.ds(0, (self.grid.count - 1) * self.band[1])]
+            pltpu.make_async_remote_copy(
+                src_ref=block, dst_ref=block, send_sem=self.send, recv_sem=self.recv.at[0],
+                device_id=self.grid.c, device_id_type=MESH,
+            ).wait_send()
+
+
+class Halves:
+    def __init__(self, grid, buffer, rows, send, recv):
+        half = rows // 2
+        self.parts = [
+            Gather(grid, buffer, rows, (i * half, half), order, send.at[i], recv.at[i])
+            for i, order in enumerate(((0, 1, 2, 3), (0, 2, 1, 3)))
+        ]
+
+    def start(self):
+        for part in self.parts:
+            part.start()
+
     def finish(self):
-        g = self.grid
         for stage in range(4):
-            earlier = [range(n) for n in g.stages[:stage]]
-            for head in itertools.product(*earlier):
-                for delta in range(1, g.stages[stage]):
-                    arrived = tuple(head) + (delta,) + (0,) * (3 - stage)
-                    block = self.block(arrived)
-                    k = self.number(arrived)
-                    pltpu.make_async_remote_copy(
-                        src_ref=block, dst_ref=block, send_sem=self.send.at[k],
-                        recv_sem=self.recv.at[k], device_id=g.c, device_id_type=MESH,
-                    ).wait_recv()
-                    self.forward(arrived, stage + 1)
+            for part in self.parts:
+                part.finish(stage)
 
     def drain(self):
-        for c in self.sent:
-            c.wait_send()
-
-
-def map_kernel(sizes, own_ref, all_ref, send, recv):
-    grid = Grid(sizes)
-    rows = own_ref.shape[0]
-    all_ref[pl.ds(grid.linear(grid.place) * rows, rows), :] = own_ref[...]
-    grid.barrier()
-    gather = Gather(grid, all_ref, rows, send, recv)
-    gather.start()
-    gather.finish()
-    gather.drain()
+        for part in self.parts:
+            part.drain()
 
 
 def split(value):
@@ -182,7 +197,7 @@
     def step(i, carry):
         first = pl.multiple_of(i * unroll, unroll)
         for j in range(unroll):
-            row = index[base + first + j]
+            row = index[base, first + j] if len(index.shape) == 2 else index[base + first + j]
             target[pl.ds(first + j, 1), :] = source[pl.ds(row, 1), :]
         return carry
 
@@ -191,26 +206,37 @@
 
 def main_kernel(
     sizes, face,
-    slots, places, own_map, all_map,
-    loads, start, basis, basis_t, weight, schur, inverse, coarse_t,
+    slots, places, own_map,
+    loads, start, basis, weight, map_block, schur, inverse, coarse_inv,
     solution, residual,
     full, s_high, s_low, b_high, b_low, m_high, m_low, t_high, t_low,
-    c_high, c_low, picked, field, local, moved, both, term_both, sol_both, coarse_rows,
+    c_high, c_low, coarse_own, coarse_t, map_all, map_rows, all_map, picked, field, moved, both, term_both, sol_both, coarse_rows,
     faces, arrived, term_all, sol_all,
-    load_sem, face_send, face_recv, term_send, term_recv, sol_send, sol_recv,
+    load_sem, map_send, map_recv, face_send, face_recv, term_send, term_recv, sol_send, sol_recv,
 ):
     grid = Grid(sizes)
     unknowns, cases = start.shape
     primal = basis.shape[1]
     own = coarse_t.shape[1]
+    local = full.at[:, 0:cases]
     load_s = pltpu.make_async_copy(schur, full, load_sem.at[0])
     load_b = pltpu.make_async_copy(inverse, full, load_sem.at[1])
     load_s.start()
+    first_own = pl.multiple_of(grid.c[2] * own, own)
+    load_c = pltpu.make_async_copy(coarse_inv.at[pl.ds(first_own, own)], coarse_own, load_sem.at[2])
+    load_c.start()
+    map_first = pl.multiple_of(grid.linear(grid.place) * 8, 8)
+    map_all[pl.ds(map_first, 8), :] = map_block[...]
     for landing in arrived:
         landing[...] = jnp.zeros_like(landing)
     grid.barrier()
+    maps = Gather(grid, map_all, 8, (0, 8), (0, 1, 2, 3), map_send, map_recv)
+    maps.start()
     split_rows(basis, m_high, m_low)
-    split_rows(basis_t, t_high, t_low)
+    for k in range(0, unknowns, primal):
+        h, l = split(basis[k : k + primal, :].T)
+        t_high[:, k : k + primal] = h
+        t_low[:, k : k + primal] = l
     solution[...] = start[...]
     sent = []
 
@@ -266,18 +292,36 @@
             load_s.wait()
             split_rows(full, s_high, s_low)
             load_b.start()
+            maps.finish(0)
 
         def stiff(r):
             field[r, :] = product(s_high[r, :], s_low[r, :], both)
 
         by_rows(unknowns, 256, stiff)
+        if iteration == 0:
+            maps.finish(1)
         exchange_start(turn)
         if iteration == 0:
+            maps.finish(2)
             load_b.wait()
             split_rows(full, b_high, b_low)
 
+            load_c.wait()
+            for k in range(0, coarse_own.shape[1], primal):
+                coarse_t[k : k + primal, :] = coarse_own[:, k : k + primal].T
+            maps.finish(3)
+
+            def pack(p, carry):
+                map_rows[pl.ds(p, 1), :] = map_all[pl.ds(p * 8, 1), :]
+                return carry
+
+            lax.fori_loop(0, grid.count, pack, 0)
+            to_scalars = pltpu.make_async_copy(map_rows, all_map, load_sem.at[3])
+            to_scalars.start()
+            to_scalars.wait()
+
             def pick(p, carry):
-                take_rows(picked, coarse_t, all_map, primal, p * primal)
+                take_rows(picked, coarse_t, all_map, primal, p)
                 h, l = split(picked[...].T)
                 k = pl.ds(pl.multiple_of(p * primal, primal), primal)
                 c_high[:, k] = h
@@ -298,7 +342,7 @@
         by_rows(unknowns, 128, settle)
         mine = pl.multiple_of(grid.linear(grid.place) * primal, primal)
         term_all[iteration, pl.ds(mine, primal), :] = product(t_high[...], t_low[...], both)
-        terms = Gather(grid, term_all.at[iteration], primal, term_send.at[iteration], term_recv.at[iteration])
+        terms = Halves(grid, term_all.at[iteration], primal, term_send.at[iteration], term_recv.at[iteration])
         terms.start()
         gathers.append(terms)
 
@@ -318,7 +362,7 @@
             return carry
 
         lax.fori_loop(0, grid.count * primal // coarse_tile, coarse, 0)
-        sols = Gather(grid, sol_all[iteration], own, sol_send.at[iteration], sol_recv.at[iteration])
+        sols = Halves(grid, sol_all[iteration], own, sol_send.at[iteration], sol_recv.at[iteration])
         sols.start()
         sols.finish()
         gathers.append(sols)
@@ -338,7 +382,7 @@
         by_rows(unknowns, 128, advance)
     for turn in range(2 * ITERS):
         exchange_drain(turn)
-    for gather in gathers:
+    for gather in gathers + [maps]:
         gather.drain()
 
 
@@ -363,16 +407,6 @@
     smem = pl.BlockSpec(memory_space=pltpu.SMEM)
     anywhere = pl.BlockSpec(memory_space=pl.ANY)
     dma = pltpu.SemaphoreType.DMA
-    maps = pl.pallas_call(
-        functools.partial(map_kernel, sizes),
-        out_shape=jax.ShapeDtypeStruct((count * 8, primal), jnp.int32),
-        in_specs=[vmem],
-        out_specs=vmem,
-        scratch_shapes=[dma((count,)), dma((count,))],
-        compiler_params=pltpu.CompilerParams(collective_id=0, has_side_effects=True),
-    )(jnp.broadcast_to(own_map[None, :], (8, primal)))
-    all_map = maps.reshape(count, 8, primal)[:, 0, :].reshape(-1)
-    own_rows = lax.dynamic_slice_in_dim(coarse_inv, lax.axis_index("gz") * own, own, 0)
     weight = jnp.broadcast_to(
         1.0 / multiplicity.reshape(unknowns, 1).astype(jnp.float32), (unknowns, cases)
     )
@@ -385,7 +419,7 @@
     solution, residual = pl.pallas_call(
         functools.partial(main_kernel, sizes, face),
         out_shape=(out, out),
-        in_specs=[smem] * 4 + [vmem] * 5 + [anywhere] * 2 + [vmem],
+        in_specs=[smem] * 3 + [vmem] * 5 + [anywhere] * 3,
         out_specs=(vmem, vmem),
         scratch_shapes=[
             pltpu.VMEM((unknowns, unknowns), f32),
@@ -399,8 +433,13 @@
             pltpu.VMEM((primal, unknowns), bf16),
             pltpu.VMEM((own, count * primal), bf16),
             pltpu.VMEM((own, count * primal), bf16),
+            pltpu.VMEM((own, total), f32),
+            pltpu.VMEM((total, own), f32),
+            pltpu.VMEM((count * 8, primal), jnp.int32),
+            pltpu.VMEM((count, primal), jnp.int32),
+            pltpu.SMEM((count, primal), jnp.int32),
             pltpu.VMEM((primal, own), f32),
-            vec, vec, vec,
+            vec, vec,
             pltpu.VMEM((unknowns, 2 * cases), bf16),
             pltpu.VMEM((coarse_tile, 2 * cases), bf16),
             pltpu.VMEM((primal, 2 * cases), bf16),
@@ -409,19 +448,20 @@
             [pltpu.VMEM((6 * face + 8, cases), f32) for _ in range(turns)],
             pltpu.VMEM((ITERS, count * primal, cases), f32),
             [pltpu.VMEM((total, cases), f32) for _ in range(ITERS)],
-            dma((2,)),
+            dma((4,)),
+            dma(()), dma((count,)),
             dma((turns, 6)), dma((turns, 6)),
-            dma((ITERS, count)), dma((ITERS, count)),
-            dma((ITERS, count)), dma((ITERS, count)),
+            dma((ITERS, 2)), dma((ITERS, 2, count)),
+            dma((ITERS, 2)), dma((ITERS, 2, count)),
         ],
         compiler_params=pltpu.CompilerParams(
             collective_id=1, has_side_effects=True, vmem_limit_bytes=67043328
         ),
     )(
-        slots, places, own_map, all_map,
+        slots, places, own_map,
         loads.reshape(unknowns, cases), start.reshape(unknowns, cases),
-        modes, modes.T, weight,
-        schur.reshape(unknowns, unknowns), inv_local.reshape(unknowns, unknowns), own_rows.T,
+        modes, weight, jnp.broadcast_to(own_map[None, :], (8, primal)),
+        schur.reshape(unknowns, unknowns), inv_local.reshape(unknowns, unknowns), coarse_inv,
     )
     return (solution.reshape(loads.shape), residual.reshape(loads.shape))
 

time: 147 us -> 132 us (0.90)
  Pallas kernels: 133 us -> 122 us
  local copies, waits for them, and re-layouts: 11.6 us -> 6.64 us
    pallas_call x1 -> x0, Pallas kernels: 16.2 us -> none  [body(): pl.pallas_call(functools.partial(map_kernel, sizes), out_shape=jax.ShapeD...]
    pallas_call x1, Pallas kernels: 117 us -> 122 us  [body(): pl.pallas_call(functools.partial(main_kernel, sizes, face), out_shape=(ou...]
    unnamed x14 -> x4, local copies, waits for them, and re-layouts: 6.62 us -> 4.33 us
    dynamic_slice x1 -> x0, local copies, waits for them, and re-layouts: 1.8 us -> none  [body(): lax.dynamic_slice_in_dim(coarse_inv, lax.axis_index('gz') * own, own, 0)]
    slice x1 -> x0, local copies, waits for them, and re-layouts: 1.51 us -> none  [body(): all_map = maps.reshape(count, 8, primal)[:, 0, :].reshape(-1)]
where the time goes in v2:
time: 132 us
  Pallas kernels  122 us (92%)
  local copies, waits for them, and re-layouts  6.64 us (5%)
  other arithmetic  2.62 us (2%)
    pallas_call x1, Pallas kernels, body(): pl.pallas_call(functools.partial(main_kernel, sizes, face), out_shape=(ou...  122 us
    unnamed x4, local copies, waits for them, and re-layouts  4.33 us

profile of v2, /device:TPU:0, one launch (start us, length us, event | category | flops | bytes accessed | tf_op | source)
XLA Modules:
  0.0 131.6 jit_solution(10310114344295187711)
XLA Ops:
  0.6 0.7 convert_divide_fusion
  1.3 1.2 broadcast_in_dim.27.map_block
  2.6 0.7 reduce
  3.3 0.1 reshape.51.slots
  3.4 0.0 copy-start
  3.4 0.6 copy-done
  4.0 0.6 select_reduce_fusion
  4.6 0.6 broadcast_add_fusion.places
  5.2 1.0 broadcast_in_dim.26.weight
  6.2 121.6 %shard_map.104 = (f32[1024,128]{1,0:T(8,128)}, f32[1024,128]{1,0:T(8,128)}) custom-call(s32[960]{0:T(1024)} %copy-done, s32[1024]{0:T(1024)} %broadcast_add_fusion.places, s32[128]{0:T(128)} %bitcast.18, f32[1024,128]{1,0:T(8,128)} %bitcast.11, f32[1024,128]{1,0:T(8,128)} %bitcast.12, f32[1024,128]{1,0:T(8,128)} %bitcast.13, ...), custom_call_target="tpu_custom_call" | custom-call | tf_op jit(solution)/shard_map/pallas_call | solution.py:419
  127.8 1.9 %copy.13 = f32[1,1,1,1024,128]{4,3,2,1,0:T(8,128)} copy(f32[1,1,1,1024,128]{4,3,2,1,0:T(8,128)} %bitcast.15) | data formatting | bytes 1048576
  129.7 1.9 %copy.14 = f32[1,1,1,1024,128]{4,3,2,1,0:T(8,128)} copy(f32[1,1,1,1024,128]{4,3,2,1,0:T(8,128)} %bitcast.14) | data formatting | bytes 1048576
  (1 shorter events, 0.0 us)
Async XLA Ops:
  3.4 0.6 copy-start
